TPU v7x, 512 devices: a whole 4x4x16 slice. The times are simulated.
512 devices in a mesh: gx: 32 (over z, core), gy: 16 (over y, x).
Axes of the slice: x: 4, y: 4, z: 16, core: 2. Of those that a mesh axis runs over, the one named last changes fastest.
Arguments:
- velocity: float32 [3, 6144, 8192], P(None, 'gx', 'gy'), may hold values from -6 to 6
- row_owner: int32 [32, 64], P('gx'), may hold values from 0 to 15, as said below
- cell_list: int32 [4, 262144], P(None, ('gx', 'gy')), may hold values from 0 to 786431
- weights: float32 [4, 262144], P(None, ('gx', 'gy')), may hold values from 0.05 to 0.5
- offsets: float32 [262144], P(('gx', 'gy')), may hold values from -0.5 to 0.5
- relax_rate: float32 [262144], P(('gx', 'gy')), may hold values from 0.05 to 0.8
- particle_velocity: float32 [3, 262144], P(None, ('gx', 'gy')), may hold values from -6 to 6
- live_counts: int32 [2048], P(('gx', 'gy')), may hold values from 1 to 128, as said below
Outputs:
- gradient: float32 [3, 6144, 8192], P(None, 'gx', 'gy')
- fluid_at_particle: float32 [3, 262144], P(None, ('gx', 'gy'))
- updated_velocity: float32 [3, 262144], P(None, ('gx', 'gy'))
Inputs may be any that keep to these rules, and one draw needn't show every extreme that they name: `row_owner`: for every gx index and every gy index, at most 2 of that device's 4 row blocks name one owner; in every row of devices along gy one owner is named by exactly 2 blocks of every device; every owner is named by some block of the row. `live_counts`: the live particles of a block are its first slots.
All inputs are finite; a program needn't handle non-finite values.
Results may differ from a plain program's by a relative error of at most 0.0029.
Values may be sent and summed in bfloat16 or wider, within the bound.
A program may use at most 128 MiB of HBM per device.

v0:
```python
import math
import jax
import jax.numpy as jnp
from jax import lax
from jax.sharding import PartitionSpec as P

ROWB = 128
PSIZE = 128
R_DECAY = (3.0 - math.sqrt(5.0)) / 2.0
A_COEF = 14.0 / 9.0
B_COEF = 1.0 / 9.0
PRECISION_HIGH = lax.Precision.HIGHEST


def extended(cells, sides, width):
    for axis, dim in sides:
        count = lax.axis_size(axis)
        head = lax.slice_in_dim(cells, 0, width, axis=dim)
        tail = lax.slice_in_dim(cells, cells.shape[dim] - width, cells.shape[dim], axis=dim)
        cells = jnp.concatenate(
            [
                lax.ppermute(tail, axis, [(i, (i + 1) % count) for i in range(count)]),
                cells,
                lax.ppermute(head, axis, [((i + 1) % count, i) for i in range(count)]),
            ],
            axis=dim,
        )
    return cells


def stencil_sum(values, weights, offsets):
    carried = values[:3].astype(jnp.float32)
    slopes = values[3:].astype(jnp.float32)
    return jnp.sum(weights[None] * (carried + offsets[None, None] * slopes), 1)


def pick_cells(table, row_ids, line_ids):
    row_width = table.shape[2]
    picked = jnp.take(table, row_ids.reshape(-1), axis=1)
    select = jnp.arange(row_width)[None, :] == line_ids.reshape(-1)[:, None]
    values = jnp.sum(jnp.where(select[None], picked, jnp.zeros((), table.dtype)), -1)
    return values.reshape((table.shape[0],) + row_ids.shape)


def signed_power(exponent):
    parity = 1.0 - 2.0 * (exponent % 2).astype(jnp.float32)
    return parity * R_DECAY ** exponent.astype(jnp.float32)


def triangle(x_cells, backward):
    position = jnp.arange(x_cells)
    distance = position[:, None] - position[None, :]
    if backward:
        distance = -distance
    return jnp.where(distance >= 0, signed_power(jnp.abs(distance)), 0.0)


def widened_solve(velocity):
    components, x_cells, local_lines = velocity.shape
    margin = 20
    extent = x_cells + 2 * margin
    padded = extended(velocity, (("gx", 1),), margin + 2)
    right_side = 0.5 * A_COEF * (
        padded[:, 3 : extent + 3] - padded[:, 1 : extent + 1]
    ) + 0.25 * B_COEF * (padded[:, 4 : extent + 4] - padded[:, 0:extent])
    forward = jnp.einsum(
        "ij,cjl->cil", triangle(extent, False), right_side, precision=PRECISION_HIGH
    )
    backward = jnp.einsum("ij,cjl->cil", triangle(extent, True), forward, precision=PRECISION_HIGH)
    return 3.0 * R_DECAY * backward[:, margin : margin + x_cells]


def per_device(
    velocity, row_owner, cell_list, weights, offsets, relax_rate, particle_velocity, live_counts
):
    components, x_cells, local_lines = velocity.shape
    gradient = widened_solve(velocity)
    fields = jnp.concatenate([velocity, gradient], 0).astype(jnp.bfloat16)
    my_owner = lax.axis_index("gy")
    owners = lax.axis_size("gy")
    block_total = local_lines // ROWB
    capacity = block_total // 2
    column = row_owner[0]
    x_index = cell_list % x_cells
    remainder = cell_list // x_cells
    line_index = remainder % ROWB
    slot_ids = remainder // ROWB
    own_routes = lax.dynamic_slice_in_dim(column, my_owner * block_total, block_total)
    ordinal = jnp.arange(block_total)
    earlier_same = (own_routes[:, None] == own_routes[None, :]) & (
        ordinal[None, :] < ordinal[:, None]
    )
    ranking = jnp.sum(earlier_same.astype(jnp.int32), 1)
    slot_index = own_routes * capacity + ranking
    matches = (slot_index[None, :] == jnp.arange(owners * capacity)[:, None]).astype(jnp.bfloat16)
    blocked = fields.reshape(6, x_cells, block_total, ROWB)
    outgoing = jnp.einsum("ckbr,sb->cksr", blocked, matches, preferred_element_type=jnp.bfloat16)
    outgoing = outgoing.reshape(6, x_cells, owners, capacity, ROWB)
    arrived = lax.all_to_all(outgoing, "gy", split_axis=2, concat_axis=2, tiled=True)
    table = arrived.reshape(6, x_cells * owners * capacity, ROWB)
    row_ids = x_index * (owners * capacity) + slot_ids
    raw = stencil_sum(pick_cells(table, row_ids, line_index), weights, offsets)
    particle_slots = weights.shape[1]
    alive = (jnp.arange(PSIZE)[None, :] < live_counts[:, None]).reshape(particle_slots)
    fluid_at_particle = jnp.where(alive[None], raw, 0.0)
    updated_velocity = jnp.where(
        alive[None],
        particle_velocity + relax_rate[None] * (fluid_at_particle - particle_velocity),
        particle_velocity,
    )
    return (gradient, fluid_at_particle, updated_velocity)


def solution(mesh):
    return jax.shard_map(
        per_device,
        mesh=mesh,
        in_specs=(
            P(None, "gx", "gy"),
            P("gx", None),
            P(None, ("gx", "gy")),
            P(None, ("gx", "gy")),
            P(("gx", "gy")),
            P(("gx", "gy")),
            P(None, ("gx", "gy")),
            P(("gx", "gy")),
        ),
        out_specs=(P(None, "gx", "gy"), P(None, ("gx", "gy")), P(None, ("gx", "gy"))),
        check_vma=False,
    )
```

profile of v0, /device:TPU:417, one launch (start us, length us, event | category | flops | bytes accessed | tf_op | source)
XLA Modules:
  0.0 247.8 jit_solution(14806160395370510572)
XLA Ops:
  0.6 1.0 fusion.99
  1.7 1.3 collective-permute-start
  3.0 1.4 convert.11
  4.5 0.2 convert_reduce_fusion
  4.7 0.1 concatenate.13
  4.9 0.2 collective-permute-done
  5.1 2.5 collective-permute-done.1
  7.5 0.2 pad_maximum_fusion
  7.7 2.0 convolution_bitcast_fusion.1
  9.8 1.5 convolution_bitcast_fusion
  11.3 1.2 fusion.98
  12.6 0.1 concatenate.14
  12.7 3.1 %fusion.7 = bf16[32,6,192,128]{3,0,2,1:T(8,128)(2,1)S(1)} fusion(bf16[3,192,4,128]{3,2,1,0:T(4,128)(2,1)S(1)} %concatenate.14, bf16[3,192,4,128]{3,2,1,0:T(4,128)(2,1)S(1)} %concatenate.13, s32[4]{0:T(128)S(1)} %fusion.79), kind=kOutput, calls=%fused_computation.13 | convolution fusion | flops 40108160 | bytes 10616848 | tf_op jit(solution)/shard_map/ckbr,sb->cksr/dot_general | solution.py:97
  15.8 10.2 %copy.30 = bf16[6,192,16,2,128]{4,3,1,0,2:T(2,128)(2,1)} copy(bf16[6,192,16,2,128]{4,3,2,1,0:T(2,128)(2,1)S(1)} %bitcast.45) | data formatting | bytes 18874368 | tf_op jit(solution)/shard_map/reshape | solution.py:98
  26.0 6.9 %all-to-all-start = ((bf16[6,192,16,2,128]{4,3,1,0,2:T(2,128)(2,1)}), bf16[6,192,16,2,128]{4,3,1,0,2:T(2,128)(2,1)}, u32[]{:S(2)}, u32[]{:S(2)}) async-start(bf16[6,192,16,2,128]{4,3,1,0,2:T(2,128)(2,1)} %copy.30), calls=%async_computation | async-start | bytes 18874368 | tf_op jit(solution)/shard_map/all_to_all | solution.py:99
  33.2 0.3 iota_compare_fusion
  33.5 144.0 %all-to-all-done = bf16[6,192,16,2,128]{4,3,1,0,2:T(2,128)(2,1)} async-done(((bf16[6,192,16,2,128]{4,3,1,0,2:T(2,128)(2,1)}), bf16[6,192,16,2,128]{4,3,1,0,2:T(2,128)(2,1)}, u32[]{:S(2)}, u32[]{:S(2)}) %all-to-all-start) | async-done | bytes 9437216 | tf_op jit(solution)/shard_map/all_to_all | solution.py:99
  177.6 19.0 %copy.31 = bf16[6,192,16,2,128]{4,0,3,2,1:T(8,128)(2,1)} copy(bf16[6,192,16,2,128]{4,3,1,0,2:T(2,128)(2,1)} %all-to-all-done) | data formatting | bytes 18874368 | tf_op jit(solution)/shard_map/all_to_all | solution.py:99
  196.6 19.3 %gather_fusion = bf16[2048,6,128]{2,1,0:T(8,128)(2,1)} fusion(bf16[6,6144,128]{2,0,1:T(8,128)(2,1)} %bitcast.46, s32[2048]{0:T(1024)S(1)} %broadcast_clamp_fusion), kind=kCustom, calls=%fused_computation | custom fusion | bytes 6299648 | tf_op jit(solution)/shard_map/jit(_take)/gather | solution.py:39
  215.9 30.1 %select_reduce_fusion = bf16[2048,6]{1,0:T(8,128)(2,1)S(1)} fusion(bf16[2048,6,128]{2,1,0:T(8,128)(2,1)} %gather_fusion, pred[2048]{0:T(1024)(128)(4,1)S(1)} %compare_and_fusion, pred[2048,128]{1,0:T(8,128)(4,1)S(1)} %iota_compare_fusion), kind=kLoop, calls=%fused_computation.1 | loop fusion | flops 4706304 | bytes 3434496 | tf_op jit(solution)/shard_map/reduce_sum | solution.py:41
  246.0 0.2 fusion.100
  246.2 0.4 copy-done.1
  246.7 0.4 fusion.13
  247.2 0.6 add_select_fusion.2
  (27 shorter events, 0.5 us)
Async XLA Ops:
  0.6 3.8 %copy-start.6 = (s32[1,64]{1,0:T(1,128)S(1)}, s32[1,64]{1,0:T(1,128)}, u32[]{:S(2)}) copy-start(s32[1,64]{1,0:T(1,128)} %param.9) | copy-start | bytes 772
  1.7 3.4 %collective-permute-start = (f32[3,22,512]{2,1,0:T(8,128)S(1)}, f32[3,22,512]{2,1,0:T(8,128)S(1)}, u32[]{:S(2)}, u32[]{:S(2)}) collective-permute-start(f32[3,22,512]{2,1,0:T(8,128)S(1)} %get-tuple-element.13), channel_id=1, source_target_pairs={{0,16},{16,32},{32,48},{48,64},{64,80},{80,96},{96,112},{112,128},... | collective-permute-start | bytes 405512 | tf_op jit(solution)/shard_map/ppermute | solution.py:22
  3.0 4.6 %collective-permute-start.1 = (f32[3,22,512]{2,1,0:T(8,128)S(1)}, f32[3,22,512]{2,1,0:T(8,128)S(1)}, u32[]{:S(2)}, u32[]{:S(2)}) collective-permute-start(f32[3,22,512]{2,1,0:T(8,128)S(1)} %get-tuple-element.14), channel_id=1, source_target_pairs={{16,0},{32,16},{48,32},{64,48},{80,64},{96,80},{112,96},{128,112},... | collective-permute-start | bytes 405512 | tf_op jit(solution)/shard_map/ppermute | solution.py:24
  3.0 4.6 %copy-start = (f32[3,192,512]{2,1,0:T(8,128)S(1)}, f32[3,192,512]{2,1,0:T(8,128)}, u32[]{:S(2)}) copy-start(f32[3,192,512]{2,1,0:T(8,128)} %param.8) | copy-start | bytes 3538948
  26.0 7.0 %copy-start.2 = (s32[4,512]{1,0:T(4,128)S(1)}, s32[4,512]{1,0:T(4,128)}, u32[]{:S(2)}) copy-start(s32[4,512]{1,0:T(4,128)} %param.10) | copy-start | bytes 24580
  26.0 7.0 %copy-start.7 = (s32[4]{0:T(128)S(1)}, s32[4]{0:T(128)}, u32[]{:S(2)}) copy-start(s32[4]{0:T(128)} %param.15) | copy-start | bytes 52
  26.0 151.5 %all-to-all-start = ((bf16[6,192,16,2,128]{4,3,1,0,2:T(2,128)(2,1)}), bf16[6,192,16,2,128]{4,3,1,0,2:T(2,128)(2,1)}, u32[]{:S(2)}, u32[]{:S(2)}) async-start(bf16[6,192,16,2,128]{4,3,1,0,2:T(2,128)(2,1)} %copy.30), calls=%async_computation | async-start | bytes 18874368 | tf_op jit(solution)/shard_map/all_to_all | solution.py:99
  246.0 0.7 copy-start.1
  246.0 0.7 copy-start.4
  246.0 1.2 copy-start.3
  246.0 1.2 copy-start.5
where the time goes:
time: 248 us
  waiting for transfers between devices  147 us (59%)
  local copies, waits for them, and re-layouts  50.7 us (20%)
  other arithmetic  34.7 us (14%)
  starting transfers between devices  8.25 us (3%)
  matrix products  6.66 us (3%)
    all_to_all x1, waiting for transfers between devices, per_device(): lax.all_to_all(outgoing, 'gy', split_axis=2, concat_axis=2, tiled=True)  144 us
    reduce_sum x1, other arithmetic, pick_cells(): jnp.sum(jnp.where(select[None], picked, jnp.zeros((), table.dtype)), -1)  30.1 us
    gather x1, local copies, waits for them, and re-layouts, pick_cells(): picked = jnp.take(table, row_ids.reshape(-1), axis=1)  19.3 us
    all_to_all x1, local copies, waits for them, and re-layouts, per_device(): lax.all_to_all(outgoing, 'gy', split_axis=2, concat_axis=2, tiled=True)  19 us
    reshape x1, local copies, waits for them, and re-layouts, per_device(): outgoing = outgoing.reshape(6, x_cells, owners, capacity, ROWB)  10.2 us
    all_to_all x1, starting transfers between devices, per_device(): lax.all_to_all(outgoing, 'gy', split_axis=2, concat_axis=2, tiled=True)  6.94 us
  transfers between devices with their start and end apart: 3, of which 3 were waited for; matrix products, arithmetic and copies ran while one was open for 1% of the time, Pallas kernels for 0%

commit v1 on v0

--- a/solution.py
+++ b/solution.py
@@ -96,7 +96,10 @@
     blocked = fields.reshape(6, x_cells, block_total, ROWB)
     outgoing = jnp.einsum("ckbr,sb->cksr", blocked, matches, preferred_element_type=jnp.bfloat16)
     outgoing = outgoing.reshape(6, x_cells, owners, capacity, ROWB)
-    arrived = lax.all_to_all(outgoing, "gy", split_axis=2, concat_axis=2, tiled=True)
+    arrived = jnp.concatenate(
+        lax.all_to_all(jnp.stack(jnp.split(outgoing, lax.axis_size("gy"), axis=2)), "gy", 0, 0),
+        axis=2,
+    )
     table = arrived.reshape(6, x_cells * owners * capacity, ROWB)
     row_ids = x_index * (owners * capacity) + slot_ids
     raw = stencil_sum(pick_cells(table, row_ids, line_index), weights, offsets)

time: 248 us -> 284 us (1.15)
  the two profiles are of different devices: /device:TPU:417 before, /device:TPU:193 now
where the time goes in v1:
time: 284 us
  waiting for transfers between devices  144 us (51%)
  local copies, waits for them, and re-layouts  86.7 us (31%)
  other arithmetic  36.5 us (13%)
  starting transfers between devices  9.15 us (3%)
  matrix products  6.85 us (2%)
    all_to_all x1, waiting for transfers between devices, per_device(): lax.all_to_all(jnp.stack(jnp.split(outgoing, lax.axis_size('gy'), axis=2)...  143 us
    another operation x1, local copies, waits for them, and re-layouts, per_device(): table = arrived.reshape(6, x_cells * owners * capacity, ROWB)  37 us
    reduce_sum x1, other arithmetic, pick_cells(): jnp.sum(jnp.where(select[None], picked, jnp.zeros((), table.dtype)), -1)  30.1 us
    gather x1, local copies, waits for them, and re-layouts, pick_cells(): picked = jnp.take(table, row_ids.reshape(-1), axis=1)  19.4 us
    unnamed x30, local copies, waits for them, and re-layouts  18.6 us
    reshape x1, local copies, waits for them, and re-layouts, per_device(): jnp.concatenate(lax.all_to_all(jnp.stack(jnp.split(outgoing, lax.axis_siz...  8.15 us
    all_to_all x1, starting transfers between devices, per_device(): lax.all_to_all(jnp.stack(jnp.split(outgoing, lax.axis_size('gy'), axis=2)...  6.94 us
  transfers between devices with their start and end apart: 3, of which 2 were waited for; matrix products, arithmetic and copies ran while one was open for 1% of the time, Pallas kernels for 0%

profile of v1, /device:TPU:193, one launch (start us, length us, event | category | flops | bytes accessed | tf_op | source)
XLA Modules:
  0.0 284.1 jit_solution(437558069760138243)
XLA Ops:
  1.6 2.2 collective-permute-start
  3.9 1.3 convert.11
  7.0 1.4 collective-permute-done.1
  8.4 1.4 pad_maximum_fusion
  9.9 2.0 convolution_bitcast_fusion.1
  11.9 1.5 convolution_bitcast_fusion
  13.5 1.2 fusion.114
  14.9 3.3 %fusion.7 = bf16[32,6,192,128]{3,0,2,1:T(8,128)(2,1)S(1)} fusion(bf16[3,192,4,128]{3,2,1,0:T(4,128)(2,1)S(1)} %concatenate.14, bf16[3,192,4,128]{3,2,1,0:T(4,128)(2,1)S(1)} %concatenate.13, s32[4]{0:T(128)S(1)} %fusion.95), kind=kOutput, calls=%fused_computation.13 | convolution fusion | flops 40108160 | bytes 10616848 | tf_op jit(solution)/shard_map/ckbr,sb->cksr/dot_general | solution.py:97
  18.1 1.2 fusion.31
  20.6 1.2 fusion.29
  21.8 1.2 fusion.28
  24.3 1.3 fusion.26
  25.5 1.3 fusion.25
  30.5 1.3 fusion.21
  31.7 1.2 fusion.20
  34.2 1.3 fusion.18
  35.4 1.2 fusion.17
  36.7 1.2 fusion.16
  37.9 6.9 %all-to-all-start = ((bf16[16,6,192,1,2,128]{5,4,2,1,3,0:T(2,128)(2,1)}), bf16[16,6,192,1,2,128]{5,4,2,1,3,0:T(2,128)(2,1)}, u32[]{:S(2)}, u32[]{:S(2)}) async-start(bf16[16,6,192,1,2,128]{5,4,2,1,3,0:T(2,128)(2,1)} %fusion.16), calls=%async_computation | async-start | bytes 18874368 | tf_op jit(solution)/shard_map/all_to_all | solution.py:100
  45.4 142.6 %all-to-all-done = bf16[16,6,192,1,2,128]{5,4,2,1,3,0:T(2,128)(2,1)} async-done(((bf16[16,6,192,1,2,128]{5,4,2,1,3,0:T(2,128)(2,1)}), bf16[16,6,192,1,2,128]{5,4,2,1,3,0:T(2,128)(2,1)}, u32[]{:S(2)}, u32[]{:S(2)}) %all-to-all-start) | async-done | bytes 9437216 | tf_op jit(solution)/shard_map/all_to_all | solution.py:100
  188.1 8.1 %copy.125 = bf16[6,192,16,1,2,128]{5,4,2,1,0,3:T(2,128)(2,1)S(1)} copy(bf16[6,192,16,1,2,128]{5,4,1,0,3,2:T(2,128)(2,1)} %bitcast.29) | data formatting | bytes 18874368 | tf_op jit(solution)/shard_map/reshape | solution.py:99
  196.2 37.0 %copy.126 = bf16[6,6144,128]{2,0,1:T(8,128)(2,1)} copy(bf16[6,6144,128]{2,1,0:T(8,128)(2,1)S(1)} %bitcast.158) | data formatting | bytes 18874368 | tf_op jit(solution)/shard_map/reshape;reshape | solution.py:103
  233.3 19.4 %gather_fusion = bf16[2048,6,128]{2,1,0:T(8,128)(2,1)} fusion(bf16[6,6144,128]{2,0,1:T(8,128)(2,1)} %copy.126, s32[2048]{0:T(1024)S(1)} %broadcast_clamp_fusion), kind=kCustom, calls=%fused_computation | custom fusion | bytes 6299648 | tf_op jit(solution)/shard_map/jit(_take)/gather | solution.py:39
  252.6 30.1 %select_reduce_fusion = bf16[2048,6]{1,0:T(8,128)(2,1)S(1)} fusion(bf16[2048,6,128]{2,1,0:T(8,128)(2,1)} %gather_fusion, pred[2048]{0:T(1024)(128)(4,1)S(1)} %compare_and_fusion, pred[2048,128]{1,0:T(8,128)(4,1)S(1)} %iota_compare_fusion), kind=kLoop, calls=%fused_computation.1 | loop fusion | flops 4706304 | bytes 3434496 | tf_op jit(solution)/shard_map/reduce_sum | solution.py:41
  (39 shorter events, 12.1 us)
Async XLA Ops:
  1.6 5.4 %collective-permute-start = (f32[3,22,512]{2,1,0:T(8,128)S(1)}, f32[3,22,512]{2,1,0:T(8,128)S(1)}, u32[]{:S(2)}, u32[]{:S(2)}) collective-permute-start(f32[3,22,512]{2,1,0:T(8,128)S(1)} %get-tuple-element.13), channel_id=1, source_target_pairs={{0,16},{16,32},{32,48},{48,64},{64,80},{80,96},{96,112},{112,128},... | collective-permute-start | bytes 405512 | tf_op jit(solution)/shard_map/ppermute | solution.py:22
  3.9 4.6 %collective-permute-start.1 = (f32[3,22,512]{2,1,0:T(8,128)S(1)}, f32[3,22,512]{2,1,0:T(8,128)S(1)}, u32[]{:S(2)}, u32[]{:S(2)}) collective-permute-start(f32[3,22,512]{2,1,0:T(8,128)S(1)} %get-tuple-element.14), channel_id=1, source_target_pairs={{16,0},{32,16},{48,32},{64,48},{80,64},{96,80},{112,96},{128,112},... | collective-permute-start | bytes 405512 | tf_op jit(solution)/shard_map/ppermute | solution.py:24
  37.9 7.0 %copy-start.1 = (s32[4,512]{1,0:T(4,128)S(1)}, s32[4,512]{1,0:T(4,128)}, u32[]{:S(2)}) copy-start(s32[4,512]{1,0:T(4,128)} %param.10) | copy-start | bytes 24580
  37.9 7.0 %copy-start.5 = (s32[4]{0:T(128)S(1)}, s32[4]{0:T(128)}, u32[]{:S(2)}) copy-start(s32[4]{0:T(128)} %param.15) | copy-start | bytes 52
  37.9 150.1 %all-to-all-start = ((bf16[16,6,192,1,2,128]{5,4,2,1,3,0:T(2,128)(2,1)}), bf16[16,6,192,1,2,128]{5,4,2,1,3,0:T(2,128)(2,1)}, u32[]{:S(2)}, u32[]{:S(2)}) async-start(bf16[16,6,192,1,2,128]{5,4,2,1,3,0:T(2,128)(2,1)} %fusion.16), calls=%async_computation | async-start | bytes 18874368 | tf_op jit(solution)/shard_map/all_to_all | solution.py:100
  233.3 49.6 %copy-start = (f32[4,512]{1,0:T(4,128)S(1)}, f32[4,512]{1,0:T(4,128)}, u32[]{:S(2)}) copy-start(f32[4,512]{1,0:T(4,128)} %param.11) | copy-start | bytes 24580
  233.3 49.6 %copy-start.3 = (f32[512]{0:T(512)S(1)}, f32[512]{0:T(512)}, u32[]{:S(2)}) copy-start(f32[512]{0:T(512)} %param.12) | copy-start | bytes 6148
  233.3 50.2 %copy-start.2 = (f32[3,512]{1,0:T(4,128)S(1)}, f32[3,512]{1,0:T(4,128)}, u32[]{:S(2)}) copy-start(f32[3,512]{1,0:T(4,128)} %param.14) | copy-start | bytes 18436
  233.3 50.2 %copy-start.4 = (f32[512]{0:T(512)S(1)}, f32[512]{0:T(512)}, u32[]{:S(2)}) copy-start(f32[512]{0:T(512)} %param.13) | copy-start | bytes 6148
